TPU v7x, 128 devices: a whole 4x4x4 slice. The times are simulated.
128 devices in a mesh: gx: 16 (over z, x), gy: 8 (over y, core).
Axes of the slice: x: 4, y: 4, z: 4, core: 2. Of those that a mesh axis runs over, the one named last changes fastest.
Arguments:
- positions: float32 [3, 262144], P(None, ('gx', 'gy')), may hold values from -6 to 6
- velocities: float32 [3, 262144], P(None, ('gx', 'gy')), may hold values from -6 to 6
- masses: float32 [262144], P(('gx', 'gy')), may hold values from 0.25 to 4
- labels: int32 [262144, 1], P(('gx', 'gy')), may hold values from 0 to 1023; in each aligned block of 2048 rows (0 to 2047, 2048 to 4095, ...) at most 4 rows name the same one
- owner_slot: int32 [1024], replicated, may hold values from 0 to 1023, each once
- group_cap: int32 [1024], replicated, may hold values from 512 to 4095
Outputs:
- compact_index: int32 [262144], P(('gx', 'gy'))
- potential: float32 [262144], P(('gx', 'gy'))
- binding: float32 [262144], P(('gx', 'gy'))
- catalog: float32 [4, 1024], P(None, ('gx', 'gy'))
Inputs may be any that keep to these rules, and one draw needn't show every extreme that they name: `labels`: on each device's 2048 particles no label occurs more than 4 times; some label occurs exactly 4 times in some devices' particles; every label occurs somewhere. `owner_slot` is a permutation. Group g is owned by device owner_slot[g] // 8 (devices numbered along gx then gy) as its local group owner_slot[g] % 8.
All inputs are finite; a program needn't handle non-finite values.
Results may differ from a plain program's by a relative error of at most 0.0003.
Values sent between devices are 32-bit elements; how exact they have to be, the bound alone decides.
A program may use at most 64 MiB of HBM per device.

v0:
```python
import jax
import jax.numpy as jnp
from jax import lax
from jax.sharding import PartitionSpec as P

CAP = 2048
softening_sq = 0.0025


def potential_of(group_block, live_count):
    coords = group_block[0:3]
    weights = group_block[6]
    width = min(512, CAP)
    block_count = (live_count + width - 1) // width

    def row_step(row_block, result):
        row_start = row_block * width
        near = lax.dynamic_slice_in_dim(coords, row_start, width, 1)
        row_ids = row_start + jnp.arange(width, dtype=jnp.int32)

        def column_step(column_block, accum):
            column_start = column_block * width
            other = lax.dynamic_slice_in_dim(coords, column_start, width, 1)
            other_mass = lax.dynamic_slice_in_dim(weights, column_start, width, 0)
            column_ids = column_start + jnp.arange(width, dtype=jnp.int32)
            dist_sq = jnp.sum((near[:, :, None] - other[:, None, :]) ** 2, axis=0)
            inverse = jnp.where(
                row_ids[:, None] == column_ids[None, :], 0.0, lax.rsqrt(dist_sq + softening_sq)
            )
            return accum + jnp.sum(inverse * other_mass[None, :], axis=1)

        accum = lax.fori_loop(0, block_count, column_step, jnp.zeros((width,), jnp.float32))
        return lax.dynamic_update_slice_in_dim(result, -accum / CAP, row_start, 0)

    return lax.fori_loop(0, block_count, row_step, jnp.zeros((CAP,), jnp.float32))


def owner_work(received):
    items = received.shape[0]
    member_ranks = received[:, 7, :]
    valid = member_ranks >= 0.0
    target = jnp.where(valid, member_ranks.astype(jnp.int32), CAP)
    compact = (
        jnp.zeros((items, 7, CAP), jnp.float32)
        .at[jnp.arange(items)[:, None, None], jnp.arange(7)[None, :, None], target[:, None, :]]
        .set(received[:, 0:7, :], mode="drop")
    )
    live = jnp.sum(valid, axis=1, dtype=jnp.int32)
    pot = lax.map(lambda packed: potential_of(packed[0], packed[1]), (compact, live))
    weights = compact[:, 6, :]
    mass_sum = jnp.sum(weights, axis=1)
    bulk = jnp.sum(weights[:, None, :] * compact[:, 3:6, :], axis=2) / mass_sum[:, None]
    energy = 0.5 * jnp.sum((compact[:, 3:6, :] - bulk[:, :, None]) ** 2, axis=1) + pot
    both = jnp.stack([pot, energy], axis=1)
    safe = jnp.broadcast_to(jnp.minimum(target, CAP - 1)[:, None, :], (items, 2, target.shape[1]))
    answers = jnp.where(valid[:, None, :], jnp.take_along_axis(both, safe, axis=2), 0.0)
    stats = jnp.concatenate([mass_sum[:, None] / CAP, bulk], axis=1)
    return (answers, stats)


def shards(positions, velocities, masses, labels, owner_slot, group_cap):
    label_flat = labels[:, 0]
    count_dev = label_flat.shape[0]
    ngroups = owner_slot.shape[0]
    devices = lax.axis_size(("gx", "gy"))
    owned = ngroups // devices
    most_rows = 2 * count_dev // ngroups
    width_all = devices * most_rows
    row_width = min(512, count_dev)
    row_blocks = count_dev // row_width
    group_ids = jnp.arange(ngroups, dtype=jnp.int32)
    particle_ids = jnp.arange(count_dev, dtype=jnp.int32)
    block_starts = jnp.arange(row_blocks, dtype=jnp.int32) * row_width

    def tally(row_start):
        rows_label = lax.dynamic_slice_in_dim(label_flat, row_start, row_width, 0)
        rows_ids = row_start + jnp.arange(row_width, dtype=jnp.int32)
        same = (rows_label[:, None] == label_flat[None, :]) & (
            particle_ids[None, :] < rows_ids[:, None]
        )
        earlier = jnp.sum(same, axis=1, dtype=jnp.int32)
        hits = jnp.sum(rows_label[:, None] == group_ids[None, :], axis=0, dtype=jnp.int32)
        return (earlier, hits)

    earlier, hits = lax.map(tally, block_starts)
    local_rank = earlier.reshape(count_dev)
    counts = jnp.sum(hits, axis=0, dtype=jnp.int32)
    table = lax.all_gather(counts[None, :], ("gx", "gy"), axis=0, tiled=True)
    position = lax.axis_index(("gx", "gy"))
    below = (jnp.arange(devices, dtype=jnp.int32) < position)[:, None]
    prefix = jnp.sum(jnp.where(below, table, 0), axis=0, dtype=jnp.int32)
    totals = jnp.sum(table, axis=0, dtype=jnp.int32)
    limits = jnp.minimum(group_cap, CAP)
    kept_counts = jnp.minimum(totals, limits)
    starts = jnp.cumsum(kept_counts) - kept_counts
    lookup = jnp.stack([prefix, limits, starts, owner_slot], axis=1).astype(jnp.float32)

    def fetch(row_start):
        rows_label = lax.dynamic_slice_in_dim(label_flat, row_start, row_width, 0)
        onehot = (rows_label[:, None] == group_ids[None, :]).astype(jnp.float32)
        return jnp.dot(
            onehot, lookup, precision=lax.Precision.HIGHEST, preferred_element_type=jnp.float32
        )

    fetched = lax.map(fetch, block_starts).reshape(count_dev, 4).astype(jnp.int32)
    global_rank = fetched[:, 0] + local_rank
    keep = global_rank < fetched[:, 1]
    compact_index = jnp.where(keep, fetched[:, 2] + global_rank, -1)
    owner = fetched[:, 3] // owned
    local_group = fetched[:, 3] % owned
    dest = jnp.where(keep, owner * most_rows + local_rank, width_all)
    fields = jnp.concatenate(
        [positions, velocities, masses[None, :], global_rank.astype(jnp.float32)[None, :]], axis=0
    )
    outgoing = jnp.zeros((owned, 8, width_all), jnp.float32).at[:, 7, :].set(-1.0)
    outgoing = outgoing.at[local_group[:, None], jnp.arange(8)[None, :], dest[:, None]].set(
        jnp.transpose(fields), mode="drop"
    )
    answers, stats = owner_work(
        lax.all_to_all(outgoing, ("gx", "gy"), split_axis=2, concat_axis=2, tiled=True)
    )
    returned, stats = (
        lax.all_to_all(answers, ("gx", "gy"), split_axis=2, concat_axis=2, tiled=True),
        stats,
    )
    safe_dest = jnp.minimum(dest, width_all - 1)
    values = returned[local_group, :, safe_dest]
    potential = jnp.where(keep, values[:, 0], 0.0)
    binding = jnp.where(keep, values[:, 1], 0.0)
    catalog = jnp.transpose(stats)
    return (compact_index, potential, binding, catalog)


def solution(mesh):
    return jax.shard_map(
        shards,
        mesh=mesh,
        in_specs=(
            P(None, ("gx", "gy")),
            P(None, ("gx", "gy")),
            P(("gx", "gy")),
            P(("gx", "gy"), None),
            P(),
            P(),
        ),
        out_specs=(P(("gx", "gy")), P(("gx", "gy")), P(("gx", "gy")), P(None, ("gx", "gy"))),
        check_vma=False,
    )
```

profile of v0, /device:TPU:1, one launch (start us, length us, event | category | flops | bytes accessed | tf_op | source)
XLA Modules:
  0.0 398.8 jit_solution(8188834028946037595)
XLA Ops:
  0.7 24.2 %while.85 = (s32[]{:T(128)}, s32[4,512]{1,0:T(4,128)S(1)}, s32[4,1024]{1,0:T(4,128)S(1)}, s32[4]{0:T(128)S(1)}, s32[2048]{0:T(1024)}, /*index=5*/s32[2048,1]{0,1:T(1,128)}, s32[]{:T(128)}, s32[]{:T(128)}, s32[]{:T(128)}) while((s32[]{:T(128)}, s32[4,512]{1,0:T(4,128)S(1)}, s32[4,1024]{1,0:T(4,128)S(1)}, s32[4]{0:T(128)S(1)}, ...), condition=%wide.region_3.4_spmd.clone, body=%wide.region_0.3_spmd.clone.sunk | while | flops 6814725 | bytes 39067 | solution.py:85
  4.7 1.7 convert_reduce_fusion.5
  10.7 1.7 convert_reduce_fusion.5
  16.8 1.7 convert_reduce_fusion.5
  22.8 1.7 convert_reduce_fusion.5
  24.9 39.5 %all-gather = s32[131072]{0:T(1024)S(1)} all-gather(s32[1024]{0:T(1024)S(1)} %reduce_sum.99), channel_id=2, replica_groups=mesh['gx'=16,'gy'=8] {'gx','gy'}, dimensions={0}, use_global_device_ids=true | all-gather | bytes 528384 | tf_op jit(solution)/shard_map/all_gather | solution.py:88
  65.3 17.6 %while.86 = (s32[]{:T(128)}, f32[4,512,4]{1,2,0:T(4,128)S(1)}, s32[4]{0:T(128)S(1)}, s32[2048]{0:T(1024)}, f32[1024,4]{0,1:T(4,128)S(1)}, /*index=5*/s32[]{:T(128)}, s32[]{:T(128)}, s32[]{:T(128)}) while((s32[]{:T(128)}, f32[4,512,4]{1,2,0:T(4,128)S(1)}, s32[4]{0:T(128)S(1)}, s32[2048]{0:T(1024)}, f32[1024,4]{0,1:T(4,128)S(1)}, ...), condition=%wide.region_10.11_spmd.clone, body=%wide.region_9.10_spmd.clone.sunk | while | flops 25690116 | bytes 30859 | solution.py:105
  68.6 1.1 fusion.34
  73.0 1.1 fusion.34
  77.4 1.1 fusion.34
  81.8 1.1 fusion.34
  85.2 60.4 %scatter_fusion = f32[32768]{0:T(1024)S(1)} fusion(f32[32768]{0:T(1024)S(1)} %copy-done, s32[16384]{0:T(1024)S(1)} %reshape.207, f32[16384]{0:T(1024)S(1)} %reshape.209), kind=kCustom, calls=%fused_computation.2 | custom fusion | bytes 262144
  146.4 1.7 reshape.225
  148.1 5.2 %all-to-all-start = ((f32[128,1,256]{2,1,0:T(1,128)}), f32[128,1,256]{2,1,0:T(1,128)S(1)}, u32[]{:S(2)}, u32[]{:S(2)}) async-start(f32[128,1,256]{2,1,0:T(1,128)} %reshape.225), calls=%async_computation | async-start | bytes 262144 | tf_op jit(solution)/shard_map/all_to_all | solution.py:120
  153.4 10.0 %all-to-all-done = f32[128,1,256]{2,1,0:T(1,128)S(1)} async-done(((f32[128,1,256]{2,1,0:T(1,128)}), f32[128,1,256]{2,1,0:T(1,128)S(1)}, u32[]{:S(2)}, u32[]{:S(2)}) %all-to-all-start) | async-done | bytes 131104 | tf_op jit(solution)/shard_map/all_to_all | solution.py:120
  164.8 1.1 reshape.226
  166.0 2.0 slice.104
  167.9 2.2 copy.43
  171.5 105.3 %scatter_custom_fusion.1 = f32[114688]{0:T(1024)S(1)} fusion(s32[28672]{0:T(1024)S(1)} %reshape.213, f32[28672]{0:T(1024)S(1)} %reshape.215, f32[]{:T(128)} %constant.239.clone.1), kind=kCustom, calls=%fused_computation.35 | custom fusion | bytes 458756
  277.3 20.6 %while.84 = (s32[]{:T(128)}, f32[8,2048]{1,0:T(8,128)S(1)}, s32[8]{0:T(128)S(1)}, f32[8,7,2048]{2,0,1:T(8,128)S(1)}, s32[]{:T(128)}, /*index=5*/s32[]{:T(128)}, ...) while((s32[]{:T(128)}, f32[8,2048]{1,0:T(8,128)S(1)}, ...), condition=%wide.region_21.22_spmd, body=%wide.region_14.21_spmd.sunk | while | flops 3409951 | bytes 2302925 | solution.py:49
  278.7 1.0 while.87
  281.2 1.0 while.87
  283.8 1.0 while.87
  286.4 1.0 while.87
  289.0 1.0 while.87
  291.5 1.0 while.87
  294.1 1.0 while.87
  297.9 63.1 %gather_fusion.1 = f32[8192]{0:T(1024)S(1)} fusion(f32[8,2,2048]{2,0,1:T(8,128)S(1)} %pad_maximum_fusion, s32[8192]{0:T(1024)S(1)} %bitcast.99), kind=kCustom, calls=%fused_computation.1 | custom fusion | bytes 163840 | tf_op jit(solution)/shard_map/jit(take_along_axis)/gather | solution.py:56
  362.1 4.1 %all-to-all-start.1 = ((f32[8,2,512]{0,1,2:T(2,128)}), f32[8,2,512]{0,1,2:T(2,128)S(1)}, u32[]{:S(2)}, u32[]{:S(2)}) async-start(f32[8,2,512]{0,1,2:T(2,128)} %copy.40), calls=%async_computation.1 | async-start | bytes 1048576 | tf_op jit(solution)/shard_map/all_to_all | solution.py:123
  366.8 13.0 %all-to-all-done.1 = f32[8,2,512]{0,1,2:T(2,128)S(1)} async-done(((f32[8,2,512]{0,1,2:T(2,128)}), f32[8,2,512]{0,1,2:T(2,128)S(1)}, u32[]{:S(2)}, u32[]{:S(2)}) %all-to-all-start.1) | async-done | bytes 32800 | tf_op jit(solution)/shard_map/all_to_all | solution.py:123
  379.8 3.2 copy.41
  383.0 13.0 %gather_fusion = f32[2048,2]{1,0:T(8,128)S(1)} fusion(f32[8,2,512]{1,2,0:T(8,128)S(1)} %copy.41, s32[2048]{0:T(1024)S(1)} %bitcast.100), kind=kCustom, calls=%fused_computation | custom fusion | bytes 49152 | tf_op jit(solution)/shard_map/gather | solution.py:127
  (250 shorter events, 48.1 us)
Async XLA Ops:
  0.6 64.0 %copy-start.3 = (s32[1024]{0:T(1024)S(1)}, s32[1024]{0:T(1024)}, u32[]{:S(2)}) copy-start(s32[1024]{0:T(1024)} %param.23) | copy-start | bytes 12292
  0.6 64.6 %copy-start.5 = (s32[1024]{0:T(1024)S(1)}, s32[1024]{0:T(1024)}, u32[]{:S(2)}) copy-start(s32[1024]{0:T(1024)} %param.22) | copy-start | bytes 12292
  64.5 18.7 %copy-start.8 = (s32[3]{0:T(128)S(1)}, s32[3]{0:T(128)}, u32[]{:S(2)}) copy-start(s32[3]{0:T(128)} %constant.257) | copy-start | bytes 40
  64.5 18.7 %copy-start.7 = (s32[3]{0:T(128)S(1)}, s32[3]{0:T(128)}, u32[]{:S(2)}) copy-start(s32[3]{0:T(128)} %constant.260) | copy-start | bytes 40
  82.9 1.4 copy-start.1
  82.9 1.4 copy-start.2
  82.9 1.4 copy-start.4
  83.7 1.4 copy-start
  148.1 15.3 %all-to-all-start = ((f32[128,1,256]{2,1,0:T(1,128)}), f32[128,1,256]{2,1,0:T(1,128)S(1)}, u32[]{:S(2)}, u32[]{:S(2)}) async-start(f32[128,1,256]{2,1,0:T(1,128)} %reshape.225), calls=%async_computation | async-start | bytes 262144 | tf_op jit(solution)/shard_map/all_to_all | solution.py:120
  167.9 2.5 copy-start.9
  167.9 2.6 copy-start.6
  362.1 17.7 %all-to-all-start.1 = ((f32[8,2,512]{0,1,2:T(2,128)}), f32[8,2,512]{0,1,2:T(2,128)S(1)}, u32[]{:S(2)}, u32[]{:S(2)}) async-start(f32[8,2,512]{0,1,2:T(2,128)} %copy.40), calls=%async_computation.1 | async-start | bytes 1048576 | tf_op jit(solution)/shard_map/all_to_all | solution.py:123
where the time goes:
time: 400 us; the launch traced here: 399 us
  local copies, waits for them, and re-layouts  277 us (69%)
  blocking collectives  39.5 us (10%)
  waiting for transfers between devices  22.9 us (6%)
  loops' own time  22.3 us (6%)
  other arithmetic  22.1 us (6%)
  starting transfers between devices  9.36 us (2%)
  matrix products  4.35 us (1%)
    unnamed x33, local copies, waits for them, and re-layouts  172 us
    gather x2, local copies, waits for them, and re-layouts, owner_work(): jnp.take_along_axis(both, safe, axis=2)  63.1 us
    all_gather x1, blocking collectives, shards(): table = lax.all_gather(counts[None, :], ('gx', 'gy'), axis=0, tiled=True)  39.5 us
    gather x1, local copies, waits for them, and re-layouts, shards(): values = returned[local_group, :, safe_dest]  13 us
    all_to_all x1, waiting for transfers between devices, shards(): lax.all_to_all(answers, ('gx', 'gy'), split_axis=2, concat_axis=2, tiled=...  13 us
    all_to_all x1, waiting for transfers between devices, shards(): lax.all_to_all(outgoing, ('gx', 'gy'), split_axis=2, concat_axis=2, tiled...  9.98 us
  transfers between devices with their start and end apart: 2, of which 2 were waited for; matrix products, arithmetic and copies ran while one was open for 0% of the time, Pallas kernels for 0%

commit v1 on v0

--- a/solution.py
+++ b/solution.py
@@ -85,7 +85,9 @@
     earlier, hits = lax.map(tally, block_starts)
     local_rank = earlier.reshape(count_dev)
     counts = jnp.sum(hits, axis=0, dtype=jnp.int32)
-    table = lax.all_gather(counts[None, :], ("gx", "gy"), axis=0, tiled=True)
+    x = counts[None, :]
+    sent = jnp.stack([x] * lax.axis_size(("gx", "gy")))
+    table = jnp.concatenate(lax.all_to_all(sent, ("gx", "gy"), 0, 0), axis=0)
     position = lax.axis_index(("gx", "gy"))
     below = (jnp.arange(devices, dtype=jnp.int32) < position)[:, None]
     prefix = jnp.sum(jnp.where(below, table, 0), axis=0, dtype=jnp.int32)

time: 400 us -> 386 us (0.965)
  blocking collectives: 39.5 us -> 0 us
  waiting for transfers between devices: 22.9 us -> 36.5 us
  starting transfers between devices: 9.36 us -> 20.1 us
    all_gather x1 -> x0, blocking collectives: 39.5 us -> none  [shards(): table = lax.all_gather(counts[None, :], ('gx', 'gy'), axis=0, tiled=True)]
    all_to_all x0 -> x1, waiting for transfers between devices: none -> 13.5 us  [shards(): table = jnp.concatenate(lax.all_to_all(sent, ('gx', 'gy'), 0, 0), axis=0)]
    all_to_all x0 -> x1, starting transfers between devices: none -> 11.5 us  [shards(): table = jnp.concatenate(lax.all_to_all(sent, ('gx', 'gy'), 0, 0), axis=0)]
  transfers between devices with their start and end apart: 2 -> 3, of which waited for: 2 -> 3; matrix products, arithmetic and copies ran while one was open for 0% -> 0% of each run, Pallas kernels for 0% -> 0%
where the time goes in v1:
time: 386 us; the launch traced here: 385 us
  local copies, waits for them, and re-layouts  278 us (72%)
  waiting for transfers between devices  36.5 us (9%)
  other arithmetic  22.5 us (6%)
  loops' own time  22.3 us (6%)
  starting transfers between devices  20.1 us (5%)
  matrix products  4.35 us (1%)
    unnamed x33, local copies, waits for them, and re-layouts  172 us
    gather x2, local copies, waits for them, and re-layouts, owner_work(): jnp.take_along_axis(both, safe, axis=2)  63.1 us
    all_to_all x1, waiting for transfers between devices, shards(): table = jnp.concatenate(lax.all_to_all(sent, ('gx', 'gy'), 0, 0), axis=0)  13.5 us
    gather x1, local copies, waits for them, and re-layouts, shards(): values = returned[local_group, :, safe_dest]  13 us
    all_to_all x1, waiting for transfers between devices, shards(): lax.all_to_all(answers, ('gx', 'gy'), split_axis=2, concat_axis=2, tiled=...  13 us
    all_to_all x1, starting transfers between devices, shards(): table = jnp.concatenate(lax.all_to_all(sent, ('gx', 'gy'), 0, 0), axis=0)  11.5 us
    all_to_all x1, waiting for transfers between devices, shards(): lax.all_to_all(outgoing, ('gx', 'gy'), split_axis=2, concat_axis=2, tiled...  10 us
    another operation x1, loops' own time, shards(): earlier, hits = lax.map(tally, block_starts)  7.94 us
  transfers between devices with their start and end apart: 3, of which 3 were waited for; matrix products, arithmetic and copies ran while one was open for 0% of the time, Pallas kernels for 0%

profile of v1, /device:TPU:1, one launch (start us, length us, event | category | flops | bytes accessed | tf_op | source)
XLA Modules:
  0.0 385.0 jit_solution(16024207797259200826)
XLA Ops:
  0.7 24.2 %while.85 = (s32[]{:T(128)}, s32[4,512]{1,0:T(4,128)S(1)}, s32[4,1024]{1,0:T(4,128)S(1)}, s32[4]{0:T(128)S(1)}, s32[2048]{0:T(1024)}, /*index=5*/s32[2048,1]{0,1:T(1,128)}, s32[]{:T(128)}, s32[]{:T(128)}, s32[]{:T(128)}) while((s32[]{:T(128)}, s32[4,512]{1,0:T(4,128)S(1)}, s32[4,1024]{1,0:T(4,128)S(1)}, s32[4]{0:T(128)S(1)}, ...), condition=%wide.region_3.4_spmd.clone, body=%wide.region_0.3_spmd.clone.sunk | while | flops 6814725 | bytes 39067 | solution.py:85
  4.7 1.7 convert_reduce_fusion.5
  10.7 1.7 convert_reduce_fusion.5
  16.7 1.7 convert_reduce_fusion.5
  22.8 1.7 convert_reduce_fusion.5
  24.9 1.1 stack.27
  26.0 11.5 %all-to-all-start = ((s32[128,1,1024]{2,1,0:T(1,128)}), s32[128,1,1024]{2,1,0:T(1,128)S(1)}, u32[]{:S(2)}, u32[]{:S(2)}) async-start(s32[128,1,1024]{2,1,0:T(1,128)} %stack.27), calls=%async_computation | async-start | bytes 1048576 | tf_op jit(solution)/shard_map/all_to_all | solution.py:90
  37.5 13.5 %all-to-all-done = s32[128,1,1024]{2,1,0:T(1,128)S(1)} async-done(((s32[128,1,1024]{2,1,0:T(1,128)}), s32[128,1,1024]{2,1,0:T(1,128)S(1)}, u32[]{:S(2)}, u32[]{:S(2)}) %all-to-all-start) | async-done | bytes 524320 | tf_op jit(solution)/shard_map/all_to_all | solution.py:90
  52.2 17.6 %while.86 = (s32[]{:T(128)}, f32[4,512,4]{1,2,0:T(4,128)S(1)}, s32[4]{0:T(128)S(1)}, s32[2048]{0:T(1024)}, f32[1024,4]{0,1:T(4,128)S(1)}, /*index=5*/s32[]{:T(128)}, s32[]{:T(128)}, s32[]{:T(128)}) while((s32[]{:T(128)}, f32[4,512,4]{1,2,0:T(4,128)S(1)}, s32[4]{0:T(128)S(1)}, s32[2048]{0:T(1024)}, f32[1024,4]{0,1:T(4,128)S(1)}, ...), condition=%wide.region_10.11_spmd.clone, body=%wide.region_9.10_spmd.clone.sunk | while | flops 25690116 | bytes 30859 | solution.py:107
  55.5 1.1 fusion.35
  59.9 1.1 fusion.35
  64.3 1.1 fusion.35
  68.7 1.1 fusion.35
  72.1 60.4 %scatter_fusion = f32[32768]{0:T(1024)S(1)} fusion(f32[32768]{0:T(1024)S(1)} %copy-done, s32[16384]{0:T(1024)S(1)} %reshape.213, f32[16384]{0:T(1024)S(1)} %reshape.215), kind=kCustom, calls=%fused_computation.2 | custom fusion | bytes 262144
  133.3 1.7 reshape.230
  135.0 4.5 %all-to-all-start.1 = ((f32[128,1,256]{2,1,0:T(1,128)}), f32[128,1,256]{2,1,0:T(1,128)S(1)}, u32[]{:S(2)}, u32[]{:S(2)}) async-start(f32[128,1,256]{2,1,0:T(1,128)} %reshape.230), calls=%async_computation.1 | async-start | bytes 262144 | tf_op jit(solution)/shard_map/all_to_all | solution.py:122
  139.5 10.0 %all-to-all-done.1 = f32[128,1,256]{2,1,0:T(1,128)S(1)} async-done(((f32[128,1,256]{2,1,0:T(1,128)}), f32[128,1,256]{2,1,0:T(1,128)S(1)}, u32[]{:S(2)}, u32[]{:S(2)}) %all-to-all-start.1) | async-done | bytes 131104 | tf_op jit(solution)/shard_map/all_to_all | solution.py:122
  151.0 1.1 reshape.231
  152.2 2.0 slice.104
  154.1 2.2 copy.44
  157.7 105.3 %scatter_custom_fusion.1 = f32[114688]{0:T(1024)S(1)} fusion(s32[28672]{0:T(1024)S(1)} %reshape.219, f32[28672]{0:T(1024)S(1)} %reshape.221, f32[]{:T(128)} %constant.239.clone.1), kind=kCustom, calls=%fused_computation.36 | custom fusion | bytes 458756
  263.5 20.6 %while.84 = (s32[]{:T(128)}, f32[8,2048]{1,0:T(8,128)S(1)}, s32[8]{0:T(128)S(1)}, f32[8,7,2048]{2,0,1:T(8,128)S(1)}, s32[]{:T(128)}, /*index=5*/s32[]{:T(128)}, ...) while((s32[]{:T(128)}, f32[8,2048]{1,0:T(8,128)S(1)}, ...), condition=%wide.region_21.22_spmd, body=%wide.region_14.21_spmd.sunk | while | flops 3409951 | bytes 2302925 | solution.py:49
  264.9 1.0 while.87
  267.5 1.0 while.87
  270.0 1.0 while.87
  272.6 1.0 while.87
  280.3 1.0 while.87
  284.1 63.1 %gather_fusion.1 = f32[8192]{0:T(1024)S(1)} fusion(f32[8,2,2048]{2,0,1:T(8,128)S(1)} %pad_maximum_fusion, s32[8192]{0:T(1024)S(1)} %bitcast.103), kind=kCustom, calls=%fused_computation.1 | custom fusion | bytes 163840 | tf_op jit(solution)/shard_map/jit(take_along_axis)/gather | solution.py:56
  348.3 4.1 %all-to-all-start.2 = ((f32[8,2,512]{0,1,2:T(2,128)}), f32[8,2,512]{0,1,2:T(2,128)S(1)}, u32[]{:S(2)}, u32[]{:S(2)}) async-start(f32[8,2,512]{0,1,2:T(2,128)} %copy.40), calls=%async_computation.2 | async-start | bytes 1048576 | tf_op jit(solution)/shard_map/all_to_all | solution.py:125
  353.0 13.0 %all-to-all-done.2 = f32[8,2,512]{0,1,2:T(2,128)S(1)} async-done(((f32[8,2,512]{0,1,2:T(2,128)}), f32[8,2,512]{0,1,2:T(2,128)S(1)}, u32[]{:S(2)}, u32[]{:S(2)}) %all-to-all-start.2) | async-done | bytes 32800 | tf_op jit(solution)/shard_map/all_to_all | solution.py:125
  366.0 3.2 copy.41
  369.2 13.0 %gather_fusion = f32[2048,2]{1,0:T(8,128)S(1)} fusion(f32[8,2,512]{1,2,0:T(8,128)S(1)} %copy.41, s32[2048]{0:T(1024)S(1)} %bitcast.104), kind=kCustom, calls=%fused_computation | custom fusion | bytes 49152 | tf_op jit(solution)/shard_map/gather | solution.py:129
  (252 shorter events, 50.4 us)
Async XLA Ops:
  0.6 50.7 %copy-start.3 = (s32[1024]{0:T(1024)S(1)}, s32[1024]{0:T(1024)}, u32[]{:S(2)}) copy-start(s32[1024]{0:T(1024)} %param.23) | copy-start | bytes 12292
  0.6 51.5 %copy-start.5 = (s32[1024]{0:T(1024)S(1)}, s32[1024]{0:T(1024)}, u32[]{:S(2)}) copy-start(s32[1024]{0:T(1024)} %param.22) | copy-start | bytes 12292
  26.0 25.0 %all-to-all-start = ((s32[128,1,1024]{2,1,0:T(1,128)}), s32[128,1,1024]{2,1,0:T(1,128)S(1)}, u32[]{:S(2)}, u32[]{:S(2)}) async-start(s32[128,1,1024]{2,1,0:T(1,128)} %stack.27), calls=%async_computation | async-start | bytes 1048576 | tf_op jit(solution)/shard_map/all_to_all | solution.py:90
  51.4 18.7 %copy-start.8 = (s32[3]{0:T(128)S(1)}, s32[3]{0:T(128)}, u32[]{:S(2)}) copy-start(s32[3]{0:T(128)} %constant.257) | copy-start | bytes 40
  51.9 18.3 %copy-start.7 = (s32[3]{0:T(128)S(1)}, s32[3]{0:T(128)}, u32[]{:S(2)}) copy-start(s32[3]{0:T(128)} %constant.260) | copy-start | bytes 40
  69.8 1.3 copy-start.1
  69.8 1.4 copy-start.2
  69.8 1.4 copy-start.4
  70.3 1.8 copy-start
  135.0 14.6 %all-to-all-start.1 = ((f32[128,1,256]{2,1,0:T(1,128)}), f32[128,1,256]{2,1,0:T(1,128)S(1)}, u32[]{:S(2)}, u32[]{:S(2)}) async-start(f32[128,1,256]{2,1,0:T(1,128)} %reshape.230), calls=%async_computation.1 | async-start | bytes 262144 | tf_op jit(solution)/shard_map/all_to_all | solution.py:122
  154.1 2.5 copy-start.9
  154.1 2.6 copy-start.6
  348.3 17.7 %all-to-all-start.2 = ((f32[8,2,512]{0,1,2:T(2,128)}), f32[8,2,512]{0,1,2:T(2,128)S(1)}, u32[]{:S(2)}, u32[]{:S(2)}) async-start(f32[8,2,512]{0,1,2:T(2,128)} %copy.40), calls=%async_computation.2 | async-start | bytes 1048576 | tf_op jit(solution)/shard_map/all_to_all | solution.py:125
